TPU v7x, 32 devices: a whole 2x2x4 slice. The times are simulated.
32 devices in a mesh: vp: 8 (over z, x), ch: 4 (over y, core).
Axes of the slice: x: 2, y: 2, z: 4, core: 2. Of those that a mesh axis runs over, the one named last changes fastest.
Arguments:
- chol_a: bfloat16 [640, 4, 6000], P('vp', None, 'ch'), may hold values from -0.078125 to 0.078125
- chol_b: bfloat16 [6000, 8, 640], P('ch', 'vp'), may hold values from -6 to 6
- amplitudes: bfloat16 [640, 8, 640], P('vp'), may hold values from -0.0390625 to 0.0390625
- vir_a: float32 [4], replicated, may hold values from 0.2 to 3
- vir_b: float32 [8], P('vp'), may hold values from 0.2 to 3
- occ_pair: float32 [8], P('ch'), may hold values from -4 to -1
Outputs:
- increment: float32 [4, 8, 8], P(None, 'vp', 'ch')
All inputs are finite; a program needn't handle non-finite values.
Results may differ from a plain program's by a relative error of at most 0.0029.
Values may be sent and summed in bfloat16 or wider, within the bound.
No kernel may reach another device: no remote copies, remote signals or barrier semaphores. Data moves between devices by JAX's collectives and lax.ppermute only.
A program may use at most 64 MiB of HBM per device.

v0:
```python
import jax
import jax.numpy as jnp
from jax import lax
from jax.sharding import PartitionSpec as P


def body(chol_a, chol_b, amplitudes, vir_a, vir_b, occ_pair):
    nch_dev = chol_b.shape[0]
    nb_dev = chol_b.shape[1]
    vir_count = chol_b.shape[2]
    a_count = chol_a.shape[1]
    pair_count = amplitudes.shape[1]
    cholesky_right = chol_b.reshape(nch_dev, nb_dev * vir_count)
    panel_rows = lax.all_gather(chol_a, "vp", axis=0, tiled=True)
    rows_here = panel_rows.shape[0]
    v_rows = jnp.dot(
        panel_rows.reshape(rows_here * a_count, nch_dev),
        cholesky_right,
        preferred_element_type=jnp.float32,
    )
    v_all = v_rows.astype(jnp.bfloat16).reshape(rows_here, a_count * nb_dev, vir_count)
    quarter = pair_count // lax.axis_size("ch")
    own_pairs = lax.dynamic_slice_in_dim(amplitudes, lax.axis_index("ch") * quarter, quarter, 1)
    spread = lax.all_gather(own_pairs, "vp", axis=0, tiled=True)
    all_pairs = lax.all_gather(spread, "ch", axis=1, tiled=True)
    ladder = jnp.einsum("cxd,cid->xi", v_all, all_pairs, preferred_element_type=jnp.float32)
    ladder = ladder.reshape(a_count, nb_dev, pair_count)
    ladder = lax.psum_scatter(ladder, "ch", scatter_dimension=2, tiled=True)
    energy_gap = vir_a[:, None, None] + vir_b[None, :, None] - occ_pair[None, None, :]
    return ladder / energy_gap


def solution(mesh):
    return jax.shard_map(
        body,
        mesh=mesh,
        in_specs=(
            P("vp", None, "ch"),
            P("ch", "vp", None),
            P("vp", None, None),
            P(),
            P("vp"),
            P("ch"),
        ),
        out_specs=P(None, "vp", "ch"),
        check_vma=False,
    )
```

profile of v0, /device:TPU:0, one launch (start us, length us, event | category | flops | bytes accessed | tf_op | source)
XLA Modules:
  0.0 245.8 jit_solution(5086026645808385693)
XLA Ops:
  6.5 0.0 copy-start
  6.5 0.0 all-gather.6.cloned.1.call-start
  6.5 0.0 copy-start.3
  6.5 0.0 copy-start.2
  6.5 2.2 constant_dynamic-slice_fusion.1
  8.7 0.0 all-gather.6.cloned.1.call-update
  8.8 0.0 all-gather.4.cloned.1.call-start
  8.8 0.7 all-gather.4.cloned.1.call-update
  9.5 0.0 all-gather.8.cloned.1.call-start
  9.6 47.5 %all-gather.6.cloned.1.call-done = bf16[640,2,640]{2,1,0:T(2,128)(2,1)} async-done(((bf16[80,2,640]{2,1,0:T(2,128)(2,1)}), bf16[640,2,640]{2,1,0:T(2,128)(2,1)}) %all-gather.6.cloned.1.call-update) | async-done | bytes 1638416 | tf_op jit(solution)/shard_map/all_gather | solution.py:24
  57.1 2.8 %copy.13 = bf16[640,2,640]{2,0,1:T(8,128)(2,1)} copy(bf16[640,2,640]{2,1,0:T(2,128)(2,1)} %all-gather.6.cloned.1.call-done) | data formatting | bytes 3276800 | tf_op jit(solution)/shard_map/all_gather | solution.py:24
  59.9 0.0 all-gather.8.cloned.1.call-update
  60.6 0.0 copy-done.3
  60.6 0.6 dynamic-slice
  61.8 0.0 copy-done.2
  61.9 113.8 %all-gather.4.cloned.1.call-done = bf16[640,4,1500]{2,1,0:T(4,128)(2,1)} async-done(((bf16[80,4,1500]{2,1,0:T(4,128)(2,1)}), bf16[640,4,1500]{2,1,0:T(4,128)(2,1)}) %all-gather.4.cloned.1.call-update) | async-done | bytes 7680016 | tf_op jit(solution)/shard_map/all_gather | solution.py:14
  175.6 13.5 %reshape.60 = bf16[2560,1500]{1,0:T(8,128)(2,1)} reshape(bf16[640,4,1500]{2,1,0:T(4,128)(2,1)} %all-gather.4.cloned.1.call-done) | data formatting | bytes 15360000 | tf_op jit(solution)/shard_map/reshape | solution.py:17
  189.1 0.0 copy-done
  189.1 9.8 %convolution_convert_fusion = bf16[2560,640]{1,0:T(8,128)(2,1)} fusion(bf16[2560,1500]{1,0:T(8,128)(2,1)} %reshape.60, bf16[1500,1,640]{2,0,1:T(8,128)(2,1)S(1)} %copy-done), kind=kOutput, calls=%fused_computation.2 | convolution fusion | flops 4916838400 | bytes 12876800 | tf_op jit(solution)/shard_map/dot_general | solution.py:16
  198.9 6.5 %reshape.62 = bf16[640,4,640]{2,1,0:T(4,128)(2,1)} reshape(bf16[2560,640]{1,0:T(8,128)(2,1)} %convolution_convert_fusion) | data formatting | bytes 6553600 | tf_op jit(solution)/shard_map/reshape | solution.py:21
  205.4 0.0 copy-start.1
  205.4 17.9 %all-gather.8.cloned.1.call-done = bf16[640,8,640]{2,0,1:T(8,128)(2,1)} async-done(((bf16[640,2,640]{2,0,1:T(8,128)(2,1)}), bf16[640,8,640]{2,0,1:T(8,128)(2,1)}) %all-gather.8.cloned.1.call-update) | async-done | bytes 6553616 | tf_op jit(solution)/shard_map/all_gather | solution.py:25
  223.3 9.5 %fusion = f32[4,8,1]{0,1,2:T(8,128)S(1)} fusion(bf16[640,4,640]{2,1,0:T(4,128)(2,1)} %reshape.62, bf16[640,8,640]{2,0,1:T(8,128)(2,1)} %all-gather.8.cloned.1.call-done), kind=kOutput, calls=%fused_computation | convolution fusion | flops 26214400 | bytes 9830528 | tf_op jit(solution)/shard_map/cxd,cid->xi/dot_general | solution.py:26
  232.7 5.9 %all-reduce = f32[4,1,8]{0,1,2:T(1,128)S(1)} all-reduce(f32[4,1,8]{0,1,2:T(1,128)S(1)} %bitcast.13), channel_id=2, replica_groups=mesh['vp'=8,'ch'=4] {'ch'}, use_global_device_ids=true, to_apply=%region_0.0.clone | all-reduce | flops 32 | bytes 256
  238.6 0.0 copy-done.1
  238.6 0.6 subtract_divide_fusion
  (2 shorter events, 0.0 us)
Async XLA Ops:
  6.5 182.5 %copy-start = (bf16[1500,1,640]{2,0,1:T(8,128)(2,1)S(1)}, bf16[1500,1,640]{2,0,1:T(8,128)(2,1)}, u32[]{:S(2)}) copy-start(bf16[1500,1,640]{2,0,1:T(8,128)(2,1)} %param.7) | copy-start | bytes 5760004
  6.5 50.6 %all-gather.6.cloned.1.call-start = ((), (), s32[]{:S(2)}) async-start(), calls=%async_computation.1 | async-start | bytes 1843200 | tf_op jit(solution)/shard_map/all_gather | solution.py:24
  6.5 54.1 %copy-start.3 = (u32[32]{0:T(128)S(1)}, u32[32]{0:T(128)}, u32[]{:S(2)}) copy-start(u32[32]{0:T(128)} %constant.15) | copy-start | bytes 388
  6.5 55.3 %copy-start.2 = (f32[4]{0:T(128)S(1)}, f32[4]{0:T(128)}, u32[]{:S(2)}) copy-start(f32[4]{0:T(128)} %param.9) | copy-start | bytes 52
  8.8 166.9 %all-gather.4.cloned.1.call-start = ((), (), s32[]{:S(2)}) async-start(), calls=%async_computation | async-start | bytes 8847360 | tf_op jit(solution)/shard_map/all_gather | solution.py:14
  9.5 213.7 %all-gather.8.cloned.1.call-start = ((), (), s32[]{:S(2)}) async-start(), calls=%async_computation.2 | async-start | bytes 8192000 | tf_op jit(solution)/shard_map/all_gather | solution.py:25
  205.4 33.3 %copy-start.1 = (f32[2]{0:T(128)S(1)}, f32[2]{0:T(128)}, u32[]{:S(2)}) copy-start(f32[2]{0:T(128)} %param.11) | copy-start | bytes 28
Sparse Core Ops, SparseCore 0:
  9.5 47.5 all-gather.5
  59.3 116.2 all-gather.3
  177.2 46.0 all-gather.7
where the time goes:
time: 246 us
  waiting for transfers between devices  180 us (73%)
  local copies, waits for them, and re-layouts  25.6 us (10%)
  matrix products  19.3 us (8%)
  between operations  14.4 us (6%)
  blocking collectives  5.89 us (2%)
    all_gather x1, waiting for transfers between devices, body(): panel_rows = lax.all_gather(chol_a, 'vp', axis=0, tiled=True)  114 us
    all_gather x1, waiting for transfers between devices, body(): spread = lax.all_gather(own_pairs, 'vp', axis=0, tiled=True)  47.5 us
    all_gather x1, waiting for transfers between devices, body(): all_pairs = lax.all_gather(spread, 'ch', axis=1, tiled=True)  17.9 us
    reshape x1, local copies, waits for them, and re-layouts, body(): panel_rows.reshape(rows_here * a_count, nch_dev)  13.5 us
    dot_general x1, matrix products, body(): jnp.dot(panel_rows.reshape(rows_here * a_count, nch_dev), cholesky_right,...  9.8 us
    dot_general x1, matrix products, body(): jnp.einsum('cxd,cid->xi', v_all, all_pairs, preferred_element_type=jnp.fl...  9.47 us
    reshape x1, local copies, waits for them, and re-layouts, body(): v_rows.astype(jnp.bfloat16).reshape(rows_here, a_count * nb_dev, vir_count)  6.49 us
    unnamed x1, blocking collectives  5.89 us
  transfers between devices with their start and end apart: 3, of which 3 were waited for; matrix products, arithmetic and copies ran while one was open for 13% of the time, Pallas kernels for 0%

commit v1 on v0

v1 whole, which is shorter than its diff:
```python
import functools

import jax
import jax.numpy as jnp
from jax import lax
from jax.experimental import pallas as pl
from jax.experimental.pallas import tpu as pltpu
from jax.sharding import PartitionSpec as P

F32 = jnp.float32
BF16 = jnp.bfloat16
AXES = ("vp", "ch")


def gathered_body(chol_a, chol_b, amplitudes, vir_a, vir_b, occ_pair):
    nch_dev, nb_dev, vir_count = chol_b.shape
    a_count = chol_a.shape[1]
    pair_count = amplitudes.shape[1]
    cholesky_right = chol_b.reshape(nch_dev, nb_dev * vir_count)
    panel_rows = lax.all_gather(chol_a, "vp", axis=0, tiled=True)
    rows_here = panel_rows.shape[0]
    v_rows = jnp.dot(
        panel_rows.reshape(rows_here * a_count, nch_dev),
        cholesky_right,
        preferred_element_type=F32,
    )
    v_all = v_rows.astype(BF16).reshape(rows_here, a_count * nb_dev, vir_count)
    quarter = pair_count // lax.axis_size("ch")
    own_pairs = lax.dynamic_slice_in_dim(amplitudes, lax.axis_index("ch") * quarter, quarter, 1)
    spread = lax.all_gather(own_pairs, "vp", axis=0, tiled=True)
    all_pairs = lax.all_gather(spread, "ch", axis=1, tiled=True)
    ladder = jnp.einsum("cxd,cid->xi", v_all, all_pairs, preferred_element_type=F32)
    ladder = ladder.reshape(a_count, nb_dev, pair_count)
    ladder = lax.psum_scatter(ladder, "ch", scatter_dimension=2, tiled=True)
    energy_gap = vir_a[:, None, None] + vir_b[None, :, None] - occ_pair[None, None, :]
    return ladder / energy_gap


def sends(vp, ch, move):
    pairs = []
    for v in range(vp):
        for c in range(ch):
            target = move(v // 2, v % 2, c // 2, c % 2)
            if target is not None:
                z, x, y, core = target
                pairs.append((v * ch + c, (2 * z + x) * ch + 2 * y + core))
    return pairs


def along_z(table):
    return lambda z, x, y, core: (table[z], x, y, core) if z in table else None


PAIR = along_z({0: 1, 1: 0, 2: 3, 3: 2})
INWARD = along_z({0: 1, 3: 2})
OUTWARD = along_z({1: 0, 2: 3})
MIDDLE = along_z({1: 2, 2: 1})
MIRROR = along_z({0: 3, 1: 2, 2: 1, 3: 0})
FLIP_X = lambda z, x, y, core: (z, 1 - x, y, core)
FLIP_X_INNER = lambda z, x, y, core: (z, 1 - x, y, core) if z in (1, 2) else None
FLIP_Y = lambda z, x, y, core: (z, x, 1 - y, core)
FLIP_CORE = lambda z, x, y, core: (z, x, y, 1 - core)


class Loader:
    def __init__(self, sems):
        self.sems = sems
        self.count = 0
        self.pending = {}

    def start(self, dst, src):
        copy = pltpu.make_async_copy(src, dst, self.sems.at[self.count])
        copy.start()
        self.pending[id(dst)] = (copy, dst)
        self.count += 1
        return dst

    def start_either(self, dst, pred, src_true, src_false):
        sem = self.sems.at[self.count]
        pl.when(pred)(lambda: pltpu.make_async_copy(src_true, dst, sem).start())
        pl.when(jnp.logical_not(pred))(lambda: pltpu.make_async_copy(src_false, dst, sem).start())
        self.pending[id(dst)] = (pltpu.make_async_copy(src_true, dst, sem), dst)
        self.count += 1
        return dst

    def wait(self, dst):
        item = self.pending.pop(id(dst), None)
        if item is not None:
            item[0].wait()


def tile_kernel(slots, mains, nears, names, counts, *refs):
    a_count, ij_count = counts
    n_in = len(names)
    inputs = dict(zip(names, refs[:n_in]))
    out = refs[n_in]
    scratch = list(refs[n_in + 1:])
    sems = scratch.pop()
    total = scratch.pop()
    hi = scratch.pop()
    lo = scratch.pop()
    z = lax.axis_index("vp") // 2
    ch = lax.axis_index("ch")
    inner = jnp.logical_or(z == 1, z == 2)
    load = Loader(sems)
    rights = {}
    held = []
    it = iter(scratch)
    first = True
    for kind, head, tail, pieces in slots:
        item = {"kind": kind}
        for key, src in (("head", head), ("tail", tail)):
            if len(src) == 1:
                item[key] = load.start(next(it), inputs[src[0]])
            else:
                item[key] = load.start_either(next(it), inner, inputs[src[0]], inputs[src[1]])
        if first:
            for name in mains + nears:
                rights[name] = load.start(next(it), inputs[name])
            first = False
        dst = next(it)
        if kind == "own":
            item["amps"] = [load.start(dst, inputs[pieces[0]])]
        else:
            item["amps"] = []
            for m in range(4):
                views = [inputs[p[m][0]] if p[m][1] is None else inputs[p[m][0]].at[p[m][1]] for p in pieces]
                if len(views) == 1:
                    item["amps"].append(load.start(dst.at[m], views[0]))
                else:
                    item["amps"].append(load.start_either(dst.at[m], inner, views[0], views[1]))
        item["amps_ref"] = dst
        held.append(item)
    total[...] = jnp.zeros_like(total)
    quarter = hi.shape[1] // 4
    amp_rows = total.shape[2]

    def contract(stack, targets, item):
        n = len(targets)
        ref = item["amps_ref"]
        acc = None
        for m in range(4):
            if item["kind"] == "own":
                left = stack(pl.ds(quarter * m, quarter))
                right = ref[pl.ds(amp_rows * m, amp_rows), :]
            else:
                j = lax.bitwise_xor(ch, (0, 2, 1, 3)[m])
                left = stack(pl.ds(pl.multiple_of(quarter * j, quarter), quarter))
                right = ref[m]
            part = lax.dot_general(
                left.reshape(n * quarter, left.shape[-1]), right, (((1,), (1,)), ((), ())),
                preferred_element_type=F32,
            )
            acc = part if acc is None else acc + part
        for i, target in enumerate(targets):
            total[target] += acc[i * quarter:(i + 1) * quarter]

    for item in held:
        k_head = item["head"].shape[1]
        own = item["kind"] == "own"
        load.wait(item["head"])
        load.wait(item["tail"])
        for name in mains + nears:
            load.wait(rights[name])
        for dst in item["amps"]:
            load.wait(dst)
        n_main, n_near = len(mains), len(nears)

        def main_tiles(full, low, item=item, k_head=k_head):
            for i, name in enumerate(mains):
                right = rights[name]
                acc = jnp.dot(item["head"][...], right[:k_head, :], preferred_element_type=F32)
                if full:
                    acc += jnp.dot(item["tail"][...], right[k_head:, :], preferred_element_type=F32)
                top = acc.astype(BF16)
                hi[i] = top
                if low:
                    lo[i] = (acc - top.astype(F32)).astype(BF16)

        def near_tiles(item=item):
            for i, name in enumerate(nears):
                acc = jnp.dot(item["tail"][...], rights[name][...], preferred_element_type=F32)
                top = acc.astype(BF16)
                hi[n_main + i] = top
                lo[n_main + i] = (acc - top.astype(F32)).astype(BF16)

        def run(full, low, near, item=item):
            a0, a1 = (0 if full is not None else n_main), (n_main + n_near if near else n_main)
            if full is not None:
                main_tiles(full, low)
            if near:
                near_tiles()
            if a1 > a0:
                contract(lambda rows: hi[a0:a1, rows, :], list(range(a0, a1)), item)
            l0, l1 = (0 if low else n_main), (n_main + n_near if near else n_main)
            if l1 > l0:
                contract(lambda rows: lo[l0:l1, rows, :], list(range(l0, l1)), item)

        has_main = True if mains else None
        if item["kind"] == "first":
            pl.when(inner)(lambda: run(has_main, False, False))
            if mains:
                pl.when(jnp.logical_not(inner))(lambda: run(False, True, False))
        elif own:
            if mains:
                run(True, False, False)
            if nears:
                pl.when(inner)(lambda: run(None, False, True))
        else:
            pl.when(inner)(lambda: run(has_main, False, bool(nears)))
            if mains:
                pl.when(jnp.logical_not(inner))(lambda: run(False, True, False))

    n = total.shape[0]
    shape = (quarter, amp_rows)
    same_c = (
        lax.broadcasted_iota(jnp.int32, shape, 0) // a_count
        == lax.broadcasted_iota(jnp.int32, shape, 1) // ij_count
    )
    picked = jnp.where(same_c[None], total[...], 0.0)
    summed = picked.reshape(n, quarter // a_count, a_count, amp_rows).sum(1).reshape(n * a_count, amp_rows)
    fold = lax.broadcasted_iota(jnp.int32, (amp_rows, ij_count), 0) % ij_count
    fold = (fold == lax.broadcasted_iota(jnp.int32, (amp_rows, ij_count), 1)).astype(F32)
    out[...] = jnp.dot(summed, fold, precision=lax.Precision.HIGHEST, preferred_element_type=F32)


def tile_call(arrays, slots, mains, nears, counts, name):
    a_count, ij_count = counts
    names = []

    def use(n):
        if n not in names:
            names.append(n)

    scratch = []
    first = True
    for kind, head, tail, pieces in slots:
        for src in (head, tail):
            for n in src:
                use(n)
            scratch.append(pltpu.VMEM(arrays[src[0]].shape, BF16))
        if first:
            for n in mains + nears:
                use(n)
                scratch.append(pltpu.VMEM(arrays[n].shape, BF16))
            first = False
        if kind == "own":
            use(pieces[0])
            shape = arrays[pieces[0]].shape
            scratch.append(pltpu.VMEM(shape, BF16))
            quarter_rows = shape[0] // 4
        else:
            for p in pieces:
                for n, _ in p:
                    use(n)
            n, index = pieces[0][0]
            shape = arrays[n].shape if index is None else arrays[n].shape[1:]
            scratch.append(pltpu.VMEM((4,) + shape, BF16))
            quarter_rows = shape[0]
    rows = arrays[slots[0][1][0]].shape[0]
    width = arrays[(mains + nears)[0]].shape[1]
    n = len(mains) + len(nears)
    scratch += [
        pltpu.VMEM((n, rows, width), BF16),
        pltpu.VMEM((n, rows, width), BF16),
        pltpu.VMEM((n, rows // 4, quarter_rows), F32),
        pltpu.SemaphoreType.DMA((8 * len(slots) + n,)),
    ]
    out = pl.pallas_call(
        functools.partial(tile_kernel, slots, mains, nears, tuple(names), counts),
        out_shape=jax.ShapeDtypeStruct((n * a_count, ij_count), F32),
        in_specs=[pl.BlockSpec(memory_space=pl.ANY)] * len(names),
        out_specs=pl.BlockSpec(memory_space=pltpu.VMEM),
        scratch_shapes=scratch,
        name=name,
    )(*[arrays[k] for k in names])
    return out.reshape(n, a_count, ij_count)


def line_body(vp, ch, chol_a, chol_b, amplitudes, vir_a, vir_b, occ_pair):
    nch_dev, _, width = chol_b.shape
    c_dev, a_count, _ = chol_a.shape
    ij_count = amplitudes.shape[1]
    counts = (a_count, ij_count)
    k_head = nch_dev * 2 // 3 // 128 * 128 + (128 if nch_dev * 2 // 3 % 128 > 64 else 0)
    where = lax.axis_index("ch")

    def go(name, value, move):
        with jax.named_scope(name):
            return lax.ppermute(value, AXES, sends(vp, ch, move))

    arr = {}
    rights = chol_b.reshape(nch_dev, width)
    arr["b"] = rights
    arr["bx"] = go("bx", rights, FLIP_X)
    q_rows = c_dev // 4
    own_quarter = lax.dynamic_slice_in_dim(amplitudes, where * q_rows, q_rows, 0).reshape(q_rows * ij_count, width)
    arr["t"] = amplitudes.reshape(c_dev * ij_count, width)
    ta = go("ta", own_quarter, PAIR)
    tb = go("tb", own_quarter, MIRROR)
    left = chol_a.reshape(c_dev * a_count, nch_dev)
    head, tail = left[:, :k_head], left[:, k_head:]
    arr["h"], arr["l"] = head, tail
    arr["h1"] = go("p1", head, PAIR)
    h2 = go("p2", head, MIDDLE)
    tc = go("tc", tb, PAIR)
    arr["t1"] = jnp.stack([ta, tb])
    arr["ty1"] = go("ty1", arr["t1"], FLIP_Y)
    arr["tk1"] = go("tk1", jnp.concatenate([arr["t1"], arr["ty1"]]), FLIP_CORE)
    h3 = go("p3", arr["h1"], MIDDLE)
    arr["near"] = go("br", rights[k_head:], INWARD)
    arr["l1"] = go("p1b", tail, INWARD)
    arr["h2i"], arr["h2o"] = h2, go("p4", h2, OUTWARD)
    arr["l2"] = go("p2b", tail, MIDDLE)
    arr["t2"] = tc
    arr["ty2"] = go("ty2", tc, FLIP_Y)
    arr["tk2"] = go("tk2", jnp.stack([tc, arr["ty2"]]), FLIP_CORE)
    arr["h3i"], arr["h3o"] = h3, go("p5", h3, OUTWARD)
    arr["l3"] = go("p3b", arr["l1"], MIDDLE)
    arr["nearx"] = go("brx", arr["near"], FLIP_X_INNER)

    p_a = (("t1", 0), ("ty1", 0), ("tk1", 0), ("tk1", 2))
    p_b = (("t1", 1), ("ty1", 1), ("tk1", 1), ("tk1", 3))
    p_c = (("t2", None), ("ty2", None), ("tk2", 0), ("tk2", 1))
    own = ("own", ("h",), ("l",), ("t",))
    slot1 = ("first", ("h1",), ("l1",), (p_a,))
    slot2 = ("far", ("h2i", "h2o"), ("l2",), (p_b, p_c))
    slot3 = ("far", ("h3i", "h3o"), ("l3",), (p_c, p_b))
    k0 = tile_call(arr, (own,), ("b",), (), counts, "k0")
    k1 = tile_call(arr, (own,), ("bx",), (), counts, "k1")
    k2 = tile_call(arr, (slot1, slot2), ("b", "bx"), (), counts, "k2")
    k3 = tile_call(arr, (slot3,), ("b", "bx"), ("near", "nearx"), counts, "k3")
    k4 = tile_call(arr, (own, slot2), (), ("near", "nearx"), counts, "k4")
    kept = jnp.concatenate([k0, k1]) + k2 + k3[:2]
    near = k3[2:] + k4
    kept = kept + go("rz", near, OUTWARD)
    ladder = kept[0] + go("rx", kept[1], FLIP_X)
    ladder = ladder + go("ry", ladder, FLIP_Y)
    ladder = ladder + go("rk", ladder, FLIP_CORE)
    pairs = ij_count // ch
    ladder = lax.dynamic_slice_in_dim(ladder, where * pairs, pairs, 1)[:, None, :]
    energy_gap = vir_a[:, None, None] + vir_b[None, :, None] - occ_pair[None, None, :]
    return ladder / energy_gap


def solution(mesh):
    vp, ch = mesh.shape["vp"], mesh.shape["ch"]
    on_line = vp == 8 and ch == 4

    def body(*args):
        if on_line:
            return line_body(vp, ch, *args)
        return gathered_body(*args)

    return jax.shard_map(
        body,
        mesh=mesh,
        in_specs=(
            P("vp", None, "ch"),
            P("ch", "vp", None),
            P("vp", None, None),
            P(),
            P("vp"),
            P("ch"),
        ),
        out_specs=P(None, "vp", "ch"),
        check_vma=False,
    )
```

time: 246 us -> 132 us (0.54)
  waiting for transfers between devices: 180 us -> 64.6 us
  starting transfers between devices: 0.08 us -> 32.3 us
  Pallas kernels: 0 us -> 25.5 us
  local copies, waits for them, and re-layouts: 25.6 us -> 5.26 us
  matrix products: 19.3 us -> 0 us
  between operations: 14.4 us -> 1.08 us
  blocking collectives: 5.89 us -> 0 us
    all_gather x3 -> x0, waiting for transfers between devices: 179 us -> none  [the longest x1 114 us: body(): panel_rows = lax.all_gather(chol_a, 'vp', axis=0, tiled=True)]
    ppermute x0 -> x22, waiting for transfers between devices: none -> 64.6 us  [go(): return lax.ppermute(value, AXES, sends(vp, ch, move))]
    ppermute x0 -> x22, starting transfers between devices: none -> 32.3 us  [go(): return lax.ppermute(value, AXES, sends(vp, ch, move))]
    pallas_call x0 -> x5, Pallas kernels: none -> 25.5 us  [tile_call(): pl.pallas_call(functools.partial(tile_kernel, slots, mains, nears, tuple(...]
    dot_general x2 -> x0, matrix products: 19.3 us -> none  [the longest x1 9.8 us: body(): jnp.dot(panel_rows.reshape(rows_here * a_count, nch_dev), cholesky_right,...]
    reshape x2, local copies, waits for them, and re-layouts: 20 us -> 2.63 us  [the longest x1 1.68 us: line_body(): left = chol_a.reshape(c_dev * a_count, nch_dev)]
    unnamed x1 -> x0, blocking collectives: 5.89 us -> none
    all_gather x1 -> x0, local copies, waits for them, and re-layouts: 2.83 us -> none  [body(): spread = lax.all_gather(own_pairs, 'vp', axis=0, tiled=True)]
  transfers between devices with their start and end apart: 3 -> 22, of which waited for: 3 -> 11; matrix products, arithmetic and copies ran while one was open for 13% -> 2% of each run, Pallas kernels for 0% -> 15%
where the time goes in v1:
time: 132 us; the launch traced here: 130 us
  waiting for transfers between devices  64.6 us (49%)
  starting transfers between devices  32.3 us (24%)
  Pallas kernels  25.5 us (19%)
  local copies, waits for them, and re-layouts  5.26 us (4%)
  other arithmetic  1.66 us (1%)
    ppermute x22, waiting for transfers between devices, go(): return lax.ppermute(value, AXES, sends(vp, ch, move))  64.6 us
    ppermute x22, starting transfers between devices, go(): return lax.ppermute(value, AXES, sends(vp, ch, move))  32.3 us
    pallas_call x5, Pallas kernels, tile_call(): pl.pallas_call(functools.partial(tile_kernel, slots, mains, nears, tuple(...  25.5 us
  transfers between devices with their start and end apart: 22, of which 11 were waited for; matrix products, arithmetic and copies ran while one was open for 2% of the time, Pallas kernels for 15%

profile of v1, /device:TPU:0, one launch (start us, length us, event | category | flops | bytes accessed | tf_op | source)
XLA Modules:
  0.0 130.5 jit_solution(5379421319138374363)
XLA Ops:
  0.0 0.9 dynamic-slice_bitcast_fusion
  1.0 5.1 %collective-permute-start.4 = (bf16[160,640]{1,0:T(8,128)(2,1)S(1)}, bf16[160,640]{1,0:T(8,128)(2,1)S(1)}, u32[]{:S(2)}, u32[]{:S(2)}) collective-permute-start(bf16[160,640]{1,0:T(8,128)(2,1)S(1)} %dynamic-slice_bitcast_fusion), channel_id=1, source_target_pairs={{0,24},{1,25},{2,26},{3,27},{4,28},{5,29},{6,30},{7,31},{8,16},{9,... | collective-permute-start | bytes 614408 | tf_op jit(solution)/shard_map/tb/ppermute | solution.py:290
  6.1 1.7 %reshape.39 = bf16[320,1500]{1,0:T(8,128)(2,1)S(1)} reshape(bf16[80,4,1500]{2,1,0:T(4,128)(2,1)} %param.6) | data formatting | bytes 1920000 | tf_op jit(solution)/shard_map/reshape | solution.py:301
  7.8 4.7 %collective-permute-start.2 = (bf16[320,476]{1,0:T(8,128)(2,1)S(1)}, bf16[320,476]{1,0:T(8,128)(2,1)}, u32[]{:S(2)}, u32[]{:S(2)}) collective-permute-start(bf16[320,476]{1,0:T(8,128)(2,1)S(1)} %slice.38.refs_1_), channel_id=1, source_target_pairs={{0,8},{1,9},{2,10},{3,11},{4,12},{5,13},{6,14},{7,15},{24,16},{25,... | collective-permute-start | bytes 913928 | tf_op jit(solution)/shard_map/p1b/ppermute | solution.py:290
  13.4 1.6 %collective-permute-start = (bf16[1500,640]{1,0:T(8,128)(2,1)S(1)}, bf16[1500,640]{1,0:T(8,128)(2,1)}, u32[]{:S(2)}, u32[]{:S(2)}) collective-permute-start(bf16[1500,640]{1,0:T(8,128)(2,1)S(1)} %bitcast.27), channel_id=1, source_target_pairs={{0,4},{1,5},{2,6},{3,7},{4,0},{5,1},{6,2},{7,3},{8,12},{9,13},{10,... | collective-permute-start | bytes 5760008 | tf_op jit(solution)/shard_map/bx/ppermute | solution.py:290
  14.9 1.0 collective-permute-done.3
  16.0 2.5 %collective-permute-start.10 = (bf16[160,640]{1,0:T(8,128)(2,1)S(1)}, bf16[160,640]{1,0:T(8,128)(2,1)S(1)}, u32[]{:S(2)}, u32[]{:S(2)}) collective-permute-start(bf16[160,640]{1,0:T(8,128)(2,1)S(1)} %collective-permute-done.4), channel_id=1, source_target_pairs={{0,8},{1,9},{2,10},{3,11},{4,12},{5,13},{6,14},{7,15},{8,0},{9,1},... | collective-permute-start | bytes 614408 | tf_op jit(solution)/shard_map/tc/ppermute | solution.py:290
  18.5 4.5 %collective-permute-done.2.refs_1_ = bf16[320,476]{1,0:T(8,128)(2,1)} collective-permute-done((bf16[320,476]{1,0:T(8,128)(2,1)S(1)}, bf16[320,476]{1,0:T(8,128)(2,1)}, u32[]{:S(2)}, u32[]{:S(2)}) %collective-permute-start.2) | collective-permute-done | bytes 304672 | tf_op jit(solution)/shard_map/p1b/ppermute | solution.py:290
  23.0 4.5 %collective-permute-start.16 = (bf16[476,640]{1,0:T(8,128)(2,1)S(1)}, bf16[476,640]{1,0:T(8,128)(2,1)S(1)}, u32[]{:S(2)}, u32[]{:S(2)}) collective-permute-start(bf16[476,640]{1,0:T(8,128)(2,1)S(1)} %slice_bitcast_fusion), channel_id=1, source_target_pairs={{0,8},{1,9},{2,10},{3,11},{4,12},{5,13},{6,14},{7,15},{24,16},{25,... | collective-permute-start | bytes 1827848 | tf_op jit(solution)/shard_map/br/ppermute | solution.py:290
  27.5 13.9 %collective-permute-done.10.refs_10_.refs_7_.refs_11_ = bf16[160,640]{1,0:T(8,128)(2,1)S(1)} collective-permute-done((bf16[160,640]{1,0:T(8,128)(2,1)S(1)}, bf16[160,640]{1,0:T(8,128)(2,1)S(1)}, u32[]{:S(2)}, u32[]{:S(2)}) %collective-permute-start.10) | collective-permute-done | bytes 204832 | tf_op jit(solution)/shard_map/tc/ppermute | solution.py:290
  41.4 1.5 %collective-permute-start.11 = (bf16[160,640]{1,0:T(8,128)(2,1)S(1)}, bf16[160,640]{1,0:T(8,128)(2,1)S(1)}, u32[]{:S(2)}, u32[]{:S(2)}) collective-permute-start(bf16[160,640]{1,0:T(8,128)(2,1)S(1)} %collective-permute-done.10.refs_10_.refs_7_.refs_11_), channel_id=1, source_target_pairs={{0,2},{1,3},{2,0},{3,1},{4,6},{5,7},{6,4},{7,5},{8,10},{9,11},{10,... | collective-permute-start | bytes 614408 | tf_op jit(solution)/shard_map/ty2/ppermute | solution.py:290
  43.7 3.6 %collective-permute-done.11.refs_11_.refs_8_.refs_12_ = bf16[160,640]{1,0:T(8,128)(2,1)S(1)} collective-permute-done((bf16[160,640]{1,0:T(8,128)(2,1)S(1)}, bf16[160,640]{1,0:T(8,128)(2,1)S(1)}, u32[]{:S(2)}, u32[]{:S(2)}) %collective-permute-start.11) | collective-permute-done | bytes 204832 | tf_op jit(solution)/shard_map/ty2/ppermute | solution.py:290
  47.4 1.5 %collective-permute-start.5 = (bf16[2,160,640]{2,1,0:T(8,128)(2,1)S(1)}, bf16[2,160,640]{2,1,0:T(8,128)(2,1)S(1)}, u32[]{:S(2)}, u32[]{:S(2)}) collective-permute-start(bf16[2,160,640]{2,1,0:T(8,128)(2,1)S(1)} %pad_maximum_fusion.1.refs_4_.refs_10_.refs_8_), channel_id=1, source_target_pairs={{0,2},{1,3},{2,0},{3,1},{4,6},{5,7},{6,4},{7,5},{8,10},{9,11},{10,... | collective-permute-start | bytes 1228808 | tf_op jit(solution)/shard_map/ty1/ppermute | solution.py:290
  48.9 1.5 %collective-permute-start.13 = (bf16[320,1024]{1,0:T(8,128)(2,1)S(1)}, bf16[320,1024]{1,0:T(8,128)(2,1)}, u32[]{:S(2)}, u32[]{:S(2)}) collective-permute-start(bf16[320,1024]{1,0:T(8,128)(2,1)S(1)} %collective-permute-done.1.refs_0_), channel_id=1, source_target_pairs={{8,16},{9,17},{10,18},{11,19},{12,20},{13,21},{14,22},{15,23},{16,... | collective-permute-start | bytes 1966088 | tf_op jit(solution)/shard_map/p3/ppermute | solution.py:290
  50.5 3.0 %collective-permute-done.16.refs_5_.refs_2_ = bf16[476,640]{1,0:T(8,128)(2,1)S(1)} collective-permute-done((bf16[476,640]{1,0:T(8,128)(2,1)S(1)}, bf16[476,640]{1,0:T(8,128)(2,1)S(1)}, u32[]{:S(2)}, u32[]{:S(2)}) %collective-permute-start.16) | collective-permute-done | bytes 609312 | tf_op jit(solution)/shard_map/br/ppermute | solution.py:290
  53.5 2.5 %collective-permute-done.5.refs_5_.refs_11_.refs_9_ = bf16[2,160,640]{2,1,0:T(8,128)(2,1)S(1)} collective-permute-done((bf16[2,160,640]{2,1,0:T(8,128)(2,1)S(1)}, bf16[2,160,640]{2,1,0:T(8,128)(2,1)S(1)}, u32[]{:S(2)}, u32[]{:S(2)}) %collective-permute-start.5) | collective-permute-done | bytes 409632 | tf_op jit(solution)/shard_map/ty1/ppermute | solution.py:290
  56.9 1.3 collective-permute-start.8
  58.2 1.3 collective-permute-start.14
  59.5 1.4 %collective-permute-start.15 = (bf16[320,476]{1,0:T(8,128)(2,1)}, bf16[320,476]{1,0:T(8,128)(2,1)}, u32[]{:S(2)}, u32[]{:S(2)}) collective-permute-start(bf16[320,476]{1,0:T(8,128)(2,1)} %collective-permute-done.2.refs_1_), channel_id=1, source_target_pairs={{8,16},{9,17},{10,18},{11,19},{12,20},{13,21},{14,22},{15,23},{16,... | collective-permute-start | bytes 913928 | tf_op jit(solution)/shard_map/p3b/ppermute | solution.py:290
  60.9 20.9 %collective-permute-done.8.refs_8_.refs_6_ = bf16[320,1024]{1,0:T(8,128)(2,1)S(1)} collective-permute-done((bf16[320,1024]{1,0:T(8,128)(2,1)S(1)}, bf16[320,1024]{1,0:T(8,128)(2,1)S(1)}, u32[]{:S(2)}, u32[]{:S(2)}) %collective-permute-start.8) | collective-permute-done | bytes 655392 | tf_op jit(solution)/shard_map/p4/ppermute | solution.py:290
  82.7 0.9 copy-done.2
  83.6 3.3 %k4.1 = f32[8,8]{1,0:T(8,128)} custom-call(bf16[320,1024]{1,0:T(8,128)(2,1)} %copy-done.1, bf16[320,476]{1,0:T(8,128)(2,1)} %copy-done.5, bf16[476,640]{1,0:T(8,128)(2,1)} %copy-done.11, bf16[476,640]{1,0:T(8,128)(2,1)} %copy-done.12, bf16[640,640]{1,0:T(8,128)(2,1)} %bitcast.28, bf16[320,1024]{1,0:T(8,128)(2,1)} %copy-done.9, bf16[320,1024]{1,0:T(8,128)(2,1)} %copy-done.10, ...), custom_call_target="tpu_custom_call" | custom-call | tf_op jit(solution)/shard_map/k4/pallas_call | solution.py:269
  86.9 8.9 %collective-permute-done.14.refs_1_ = bf16[320,1024]{1,0:T(8,128)(2,1)} collective-permute-done((bf16[320,1024]{1,0:T(8,128)(2,1)}, bf16[320,1024]{1,0:T(8,128)(2,1)}, u32[]{:S(2)}, u32[]{:S(2)}) %collective-permute-start.14) | collective-permute-done | bytes 655392 | tf_op jit(solution)/shard_map/p5/ppermute | solution.py:290
  95.7 5.7 %k3.1 = f32[16,8]{1,0:T(8,128)} custom-call(bf16[320,1024]{1,0:T(8,128)(2,1)} %collective-permute-done.13.refs_0_, bf16[320,1024]{1,0:T(8,128)(2,1)} %collective-permute-done.14.refs_1_, bf16[320,476]{1,0:T(8,128)(2,1)} %collective-permute-done.15.refs_2_, bf16[1500,640]{1,0:T(8,128)(2,1)} %bitcast.24, ...), custom_call_target="tpu_custom_call" | custom-call | tf_op jit(solution)/shard_map/k3/pallas_call | solution.py:269
  102.2 1.3 collective-permute-start.18
  103.5 4.6 %k0.1 = f32[4,8]{1,0:T(4,128)} custom-call(bf16[320,1024]{1,0:T(8,128)(2,1)} %copy-done.1, bf16[320,476]{1,0:T(8,128)(2,1)} %copy-done.5, bf16[1500,640]{1,0:T(8,128)(2,1)} %bitcast.25, bf16[640,640]{1,0:T(8,128)(2,1)} %bitcast.29), custom_call_target="tpu_custom_call" | custom-call | tf_op jit(solution)/shard_map/k0/pallas_call | solution.py:269
  108.8 7.2 %k2.1 = f32[8,8]{1,0:T(8,128)} custom-call(bf16[320,1024]{1,0:T(8,128)(2,1)} %copy-done.14, bf16[320,476]{1,0:T(8,128)(2,1)} %collective-permute-done.2.refs_1_, bf16[1500,640]{1,0:T(8,128)(2,1)} %bitcast.26, bf16[1500,640]{1,0:T(8,128)(2,1)} %collective-permute-done.refs_2_.refs_3_.refs_4_, bf16[2,160,640]{2,1,0:T(8,128)(2,1)} %copy-done.3, ...), custom_call_target="tpu_custom_call" | custom-call | tf_op jit(solution)/shard_map/k2/pallas_call | solution.py:269
  116.1 4.6 %k1.1 = f32[4,8]{1,0:T(4,128)} custom-call(bf16[320,1024]{1,0:T(8,128)(2,1)} %copy-done.1, bf16[320,476]{1,0:T(8,128)(2,1)} %copy-done.5, bf16[1500,640]{1,0:T(8,128)(2,1)} %collective-permute-done.refs_2_.refs_3_.refs_4_, bf16[640,640]{1,0:T(8,128)(2,1)} %bitcast.30), custom_call_target="tpu_custom_call" | custom-call | tf_op jit(solution)/shard_map/k1/pallas_call | solution.py:269
  121.4 1.5 %collective-permute-start.19 = (f32[4,8]{1,0:T(4,128)S(1)}, f32[4,8]{1,0:T(4,128)S(1)}, u32[]{:S(2)}, u32[]{:S(2)}) collective-permute-start(f32[4,8]{1,0:T(4,128)S(1)} %slice_bitcast_fusion.1), channel_id=1, source_target_pairs={{0,4},{1,5},{2,6},{3,7},{4,0},{5,1},{6,2},{7,3},{8,12},{9,13},{10,... | collective-permute-start | bytes 392 | tf_op jit(solution)/shard_map/rx/ppermute | solution.py:290
  122.9 2.1 %collective-permute-done.19 = f32[4,8]{1,0:T(4,128)S(1)} collective-permute-done((f32[4,8]{1,0:T(4,128)S(1)}, f32[4,8]{1,0:T(4,128)S(1)}, u32[]{:S(2)}, u32[]{:S(2)}) %collective-permute-start.19) | collective-permute-done | bytes 160 | tf_op jit(solution)/shard_map/rx/ppermute | solution.py:290
  125.5 3.1 %collective-permute-done.20 = f32[4,8]{1,0:T(4,128)S(1)} collective-permute-done((f32[4,8]{1,0:T(4,128)S(1)}, f32[4,8]{1,0:T(4,128)S(1)}, u32[]{:S(2)}, u32[]{:S(2)}) %collective-permute-start.20) | collective-permute-done | bytes 160 | tf_op jit(solution)/shard_map/ry/ppermute | solution.py:290
  128.6 1.2 collective-permute-done.21
  (74 shorter events, 6.1 us)
Async XLA Ops:
  1.0 12.4 %collective-permute-start.4 = (bf16[160,640]{1,0:T(8,128)(2,1)S(1)}, bf16[160,640]{1,0:T(8,128)(2,1)S(1)}, u32[]{:S(2)}, u32[]{:S(2)}) collective-permute-start(bf16[160,640]{1,0:T(8,128)(2,1)S(1)} %dynamic-slice_bitcast_fusion), channel_id=1, source_target_pairs={{0,24},{1,25},{2,26},{3,27},{4,28},{5,29},{6,30},{7,31},{8,16},{9,... | collective-permute-start | bytes 614408 | tf_op jit(solution)/shard_map/tb/ppermute | solution.py:290
  6.1 9.9 %collective-permute-start.3 = (bf16[160,640]{1,0:T(8,128)(2,1)S(1)}, bf16[160,640]{1,0:T(8,128)(2,1)S(1)}, u32[]{:S(2)}, u32[]{:S(2)}) collective-permute-start(bf16[160,640]{1,0:T(8,128)(2,1)S(1)} %dynamic-slice_bitcast_fusion), channel_id=1, source_target_pairs={{0,8},{1,9},{2,10},{3,11},{4,12},{5,13},{6,14},{7,15},{8,0},{9,1},... | collective-permute-start | bytes 614408 | tf_op jit(solution)/shard_map/ta/ppermute | solution.py:290
  7.8 42.6 %copy-start.5 = (bf16[320,476]{1,0:T(8,128)(2,1)}, bf16[320,476]{1,0:T(8,128)(2,1)S(1)}, u32[]{:S(2)}) copy-start(bf16[320,476]{1,0:T(8,128)(2,1)S(1)} %slice.38.refs_1_) | copy-start | bytes 913924
  7.8 15.1 %collective-permute-start.2 = (bf16[320,476]{1,0:T(8,128)(2,1)S(1)}, bf16[320,476]{1,0:T(8,128)(2,1)}, u32[]{:S(2)}, u32[]{:S(2)}) collective-permute-start(bf16[320,476]{1,0:T(8,128)(2,1)S(1)} %slice.38.refs_1_), channel_id=1, source_target_pairs={{0,8},{1,9},{2,10},{3,11},{4,12},{5,13},{6,14},{7,15},{24,16},{25,... | collective-permute-start | bytes 913928 | tf_op jit(solution)/shard_map/p1b/ppermute | solution.py:290
  12.6 44.2 %copy-start.1 = (bf16[320,1024]{1,0:T(8,128)(2,1)}, bf16[320,1024]{1,0:T(8,128)(2,1)S(1)}, u32[]{:S(2)}) copy-start(bf16[320,1024]{1,0:T(8,128)(2,1)S(1)} %slice.37.refs_0_) | copy-start | bytes 1966084
  12.6 36.3 %collective-permute-start.1 = (bf16[320,1024]{1,0:T(8,128)(2,1)S(1)}, bf16[320,1024]{1,0:T(8,128)(2,1)S(1)}, u32[]{:S(2)}, u32[]{:S(2)}) collective-permute-start(bf16[320,1024]{1,0:T(8,128)(2,1)S(1)} %slice.37.refs_0_), channel_id=1, source_target_pairs={{0,8},{1,9},{2,10},{3,11},{4,12},{5,13},{6,14},{7,15},{8,0},{9,1},... | collective-permute-start | bytes 1966088 | tf_op jit(solution)/shard_map/p1/ppermute | solution.py:290
  12.7 30.3 %collective-permute-start.9 = (bf16[320,476]{1,0:T(8,128)(2,1)S(1)}, bf16[320,476]{1,0:T(8,128)(2,1)S(1)}, u32[]{:S(2)}, u32[]{:S(2)}) collective-permute-start(bf16[320,476]{1,0:T(8,128)(2,1)S(1)} %slice.38.refs_1_), channel_id=1, source_target_pairs={{8,16},{9,17},{10,18},{11,19},{12,20},{13,21},{14,22},{15,23},{16,... | collective-permute-start | bytes 913928 | tf_op jit(solution)/shard_map/p2b/ppermute | solution.py:290
  13.4 73.5 %collective-permute-start = (bf16[1500,640]{1,0:T(8,128)(2,1)S(1)}, bf16[1500,640]{1,0:T(8,128)(2,1)}, u32[]{:S(2)}, u32[]{:S(2)}) collective-permute-start(bf16[1500,640]{1,0:T(8,128)(2,1)S(1)} %bitcast.27), channel_id=1, source_target_pairs={{0,4},{1,5},{2,6},{3,7},{4,0},{5,1},{6,2},{7,3},{8,12},{9,13},{10,... | collective-permute-start | bytes 5760008 | tf_op jit(solution)/shard_map/bx/ppermute | solution.py:290
  16.0 25.5 %collective-permute-start.10 = (bf16[160,640]{1,0:T(8,128)(2,1)S(1)}, bf16[160,640]{1,0:T(8,128)(2,1)S(1)}, u32[]{:S(2)}, u32[]{:S(2)}) collective-permute-start(bf16[160,640]{1,0:T(8,128)(2,1)S(1)} %collective-permute-done.4), channel_id=1, source_target_pairs={{0,8},{1,9},{2,10},{3,11},{4,12},{5,13},{6,14},{7,15},{8,0},{9,1},... | collective-permute-start | bytes 614408 | tf_op jit(solution)/shard_map/tc/ppermute | solution.py:290
  23.0 30.5 %collective-permute-start.16 = (bf16[476,640]{1,0:T(8,128)(2,1)S(1)}, bf16[476,640]{1,0:T(8,128)(2,1)S(1)}, u32[]{:S(2)}, u32[]{:S(2)}) collective-permute-start(bf16[476,640]{1,0:T(8,128)(2,1)S(1)} %slice_bitcast_fusion), channel_id=1, source_target_pairs={{0,8},{1,9},{2,10},{3,11},{4,12},{5,13},{6,14},{7,15},{24,16},{25,... | collective-permute-start | bytes 1827848 | tf_op jit(solution)/shard_map/br/ppermute | solution.py:290
  41.4 41.3 %copy-start.7 = (bf16[160,640]{1,0:T(8,128)(2,1)}, bf16[160,640]{1,0:T(8,128)(2,1)S(1)}, u32[]{:S(2)}) copy-start(bf16[160,640]{1,0:T(8,128)(2,1)S(1)} %collective-permute-done.10.refs_10_.refs_7_.refs_11_) | copy-start | bytes 614404
  41.4 6.0 %collective-permute-start.11 = (bf16[160,640]{1,0:T(8,128)(2,1)S(1)}, bf16[160,640]{1,0:T(8,128)(2,1)S(1)}, u32[]{:S(2)}, u32[]{:S(2)}) collective-permute-start(bf16[160,640]{1,0:T(8,128)(2,1)S(1)} %collective-permute-done.10.refs_10_.refs_7_.refs_11_), channel_id=1, source_target_pairs={{0,2},{1,3},{2,0},{3,1},{4,6},{5,7},{6,4},{7,5},{8,10},{9,11},{10,... | collective-permute-start | bytes 614408 | tf_op jit(solution)/shard_map/ty2/ppermute | solution.py:290
  42.9 13.8 %collective-permute-start.7 = (bf16[320,1024]{1,0:T(8,128)(2,1)S(1)}, bf16[320,1024]{1,0:T(8,128)(2,1)S(1)}, u32[]{:S(2)}, u32[]{:S(2)}) collective-permute-start(bf16[320,1024]{1,0:T(8,128)(2,1)S(1)} %slice.37.refs_0_), channel_id=1, source_target_pairs={{8,16},{9,17},{10,18},{11,19},{12,20},{13,21},{14,22},{15,23},{16,... | collective-permute-start | bytes 1966088 | tf_op jit(solution)/shard_map/p2/ppermute | solution.py:290
  43.7 38.9 %copy-start.3 = (bf16[2,160,640]{2,1,0:T(8,128)(2,1)}, bf16[2,160,640]{2,1,0:T(8,128)(2,1)S(1)}, u32[]{:S(2)}) copy-start(bf16[2,160,640]{2,1,0:T(8,128)(2,1)S(1)} %pad_maximum_fusion.1.refs_4_.refs_10_.refs_8_) | copy-start | bytes 1228804
  47.4 8.6 %collective-permute-start.5 = (bf16[2,160,640]{2,1,0:T(8,128)(2,1)S(1)}, bf16[2,160,640]{2,1,0:T(8,128)(2,1)S(1)}, u32[]{:S(2)}, u32[]{:S(2)}) collective-permute-start(bf16[2,160,640]{2,1,0:T(8,128)(2,1)S(1)} %pad_maximum_fusion.1.refs_4_.refs_10_.refs_8_), channel_id=1, source_target_pairs={{0,2},{1,3},{2,0},{3,1},{4,6},{5,7},{6,4},{7,5},{8,10},{9,11},{10,... | collective-permute-start | bytes 1228808 | tf_op jit(solution)/shard_map/ty1/ppermute | solution.py:290
  48.9 32.9 %copy-start.14 = (bf16[320,1024]{1,0:T(8,128)(2,1)}, bf16[320,1024]{1,0:T(8,128)(2,1)S(1)}, u32[]{:S(2)}) copy-start(bf16[320,1024]{1,0:T(8,128)(2,1)S(1)} %collective-permute-done.1.refs_0_) | copy-start | bytes 1966084
  48.9 9.3 %collective-permute-start.13 = (bf16[320,1024]{1,0:T(8,128)(2,1)S(1)}, bf16[320,1024]{1,0:T(8,128)(2,1)}, u32[]{:S(2)}, u32[]{:S(2)}) collective-permute-start(bf16[320,1024]{1,0:T(8,128)(2,1)S(1)} %collective-permute-done.1.refs_0_), channel_id=1, source_target_pairs={{8,16},{9,17},{10,18},{11,19},{12,20},{13,21},{14,22},{15,23},{16,... | collective-permute-start | bytes 1966088 | tf_op jit(solution)/shard_map/p3/ppermute | solution.py:290
  53.5 28.3 %copy-start.11 = (bf16[476,640]{1,0:T(8,128)(2,1)}, bf16[476,640]{1,0:T(8,128)(2,1)S(1)}, u32[]{:S(2)}) copy-start(bf16[476,640]{1,0:T(8,128)(2,1)S(1)} %collective-permute-done.16.refs_5_.refs_2_) | copy-start | bytes 1827844
  53.5 3.4 %collective-permute-start.12 = (bf16[2,160,640]{2,1,0:T(8,128)(2,1)S(1)}, bf16[2,160,640]{2,1,0:T(8,128)(2,1)S(1)}, u32[]{:S(2)}, u32[]{:S(2)}) collective-permute-start(bf16[2,160,640]{2,1,0:T(8,128)(2,1)S(1)} %pad_maximum_fusion.2), channel_id=1, source_target_pairs={{0,1},{1,0},{2,3},{3,2},{4,5},{5,4},{6,7},{7,6},{8,9},{9,8},{10,11... | collective-permute-start | bytes 1228808 | tf_op jit(solution)/shard_map/tk2/ppermute | solution.py:290
  56.0 25.9 %copy-start.4 = (bf16[2,160,640]{2,1,0:T(8,128)(2,1)}, bf16[2,160,640]{2,1,0:T(8,128)(2,1)S(1)}, u32[]{:S(2)}) copy-start(bf16[2,160,640]{2,1,0:T(8,128)(2,1)S(1)} %collective-permute-done.5.refs_5_.refs_11_.refs_9_) | copy-start | bytes 1228804
  56.0 3.6 %collective-permute-start.17 = (bf16[476,640]{1,0:T(8,128)(2,1)S(1)}, bf16[476,640]{1,0:T(8,128)(2,1)S(1)}, u32[]{:S(2)}, u32[]{:S(2)}) collective-permute-start(bf16[476,640]{1,0:T(8,128)(2,1)S(1)} %collective-permute-done.16.refs_5_.refs_2_), channel_id=1, source_target_pairs={{8,12},{9,13},{10,14},{11,15},{12,8},{13,9},{14,10},{15,11},{16,20... | collective-permute-start | bytes 1827848 | tf_op jit(solution)/shard_map/brx/ppermute | solution.py:290
  56.8 25.0 %copy-start.9 = (bf16[320,1024]{1,0:T(8,128)(2,1)}, bf16[320,1024]{1,0:T(8,128)(2,1)S(1)}, u32[]{:S(2)}) copy-start(bf16[320,1024]{1,0:T(8,128)(2,1)S(1)} %collective-permute-done.7.refs_7_.refs_5_) | copy-start | bytes 1966084
  56.8 25.0 %collective-permute-start.6 = (bf16[4,160,640]{2,1,0:T(8,128)(2,1)S(1)}, bf16[4,160,640]{2,1,0:T(8,128)(2,1)S(1)}, u32[]{:S(2)}, u32[]{:S(2)}) collective-permute-start(bf16[4,160,640]{2,1,0:T(8,128)(2,1)S(1)} %pad_maximum_fusion), channel_id=1, source_target_pairs={{0,1},{1,0},{2,3},{3,2},{4,5},{5,4},{6,7},{7,6},{8,9},{9,8},{10,11... | collective-permute-start | bytes 2457608 | tf_op jit(solution)/shard_map/tk1/ppermute | solution.py:290
  56.9 24.9 %copy-start.6 = (bf16[2,160,640]{2,1,0:T(8,128)(2,1)}, bf16[2,160,640]{2,1,0:T(8,128)(2,1)S(1)}, u32[]{:S(2)}) copy-start(bf16[2,160,640]{2,1,0:T(8,128)(2,1)S(1)} %collective-permute-done.12.refs_12_.refs_9_.refs_13_) | copy-start | bytes 1228804
  56.9 24.9 %collective-permute-start.8 = (bf16[320,1024]{1,0:T(8,128)(2,1)S(1)}, bf16[320,1024]{1,0:T(8,128)(2,1)S(1)}, u32[]{:S(2)}, u32[]{:S(2)}) collective-permute-start(bf16[320,1024]{1,0:T(8,128)(2,1)S(1)} %collective-permute-done.7.refs_7_.refs_5_), channel_id=1, source_target_pairs={{8,0},{9,1},{10,2},{11,3},{12,4},{13,5},{14,6},{15,7},{16,24},{17,... | collective-permute-start | bytes 1966088 | tf_op jit(solution)/shard_map/p4/ppermute | solution.py:290
  58.2 37.5 %collective-permute-start.14 = (bf16[320,1024]{1,0:T(8,128)(2,1)}, bf16[320,1024]{1,0:T(8,128)(2,1)}, u32[]{:S(2)}, u32[]{:S(2)}) collective-permute-start(bf16[320,1024]{1,0:T(8,128)(2,1)} %collective-permute-done.13.refs_0_), channel_id=1, source_target_pairs={{8,0},{9,1},{10,2},{11,3},{12,4},{13,5},{14,6},{15,7},{16,24},{17,... | collective-permute-start | bytes 1966088 | tf_op jit(solution)/shard_map/p5/ppermute | solution.py:290
  59.5 22.3 %copy-start.12 = (bf16[476,640]{1,0:T(8,128)(2,1)}, bf16[476,640]{1,0:T(8,128)(2,1)S(1)}, u32[]{:S(2)}) copy-start(bf16[476,640]{1,0:T(8,128)(2,1)S(1)} %collective-permute-done.17.refs_6_.refs_3_) | copy-start | bytes 1827844
  59.5 27.3 %collective-permute-start.15 = (bf16[320,476]{1,0:T(8,128)(2,1)}, bf16[320,476]{1,0:T(8,128)(2,1)}, u32[]{:S(2)}, u32[]{:S(2)}) collective-permute-start(bf16[320,476]{1,0:T(8,128)(2,1)} %collective-permute-done.2.refs_1_), channel_id=1, source_target_pairs={{8,16},{9,17},{10,18},{11,19},{12,20},{13,21},{14,22},{15,23},{16,... | collective-permute-start | bytes 913928 | tf_op jit(solution)/shard_map/p3b/ppermute | solution.py:290
  102.2 18.5 %collective-permute-start.18 = (f32[2,4,8]{2,1,0:T(4,128)S(1)}, f32[2,4,8]{2,1,0:T(4,128)S(1)}, u32[]{:S(2)}, u32[]{:S(2)}) collective-permute-start(f32[2,4,8]{2,1,0:T(4,128)S(1)} %bitcast.41), channel_id=1, source_target_pairs={{8,0},{9,1},{10,2},{11,3},{12,4},{13,5},{14,6},{15,7},{16,24},{17,... | collective-permute-start | bytes 776 | tf_op jit(solution)/shard_map/rz/ppermute | solution.py:290
  121.4 3.6 %collective-permute-start.19 = (f32[4,8]{1,0:T(4,128)S(1)}, f32[4,8]{1,0:T(4,128)S(1)}, u32[]{:S(2)}, u32[]{:S(2)}) collective-permute-start(f32[4,8]{1,0:T(4,128)S(1)} %slice_bitcast_fusion.1), channel_id=1, source_target_pairs={{0,4},{1,5},{2,6},{3,7},{4,0},{5,1},{6,2},{7,3},{8,12},{9,13},{10,... | collective-permute-start | bytes 392 | tf_op jit(solution)/shard_map/rx/ppermute | solution.py:290
  125.0 3.6 %collective-permute-start.20 = (f32[4,8]{1,0:T(4,128)S(1)}, f32[4,8]{1,0:T(4,128)S(1)}, u32[]{:S(2)}, u32[]{:S(2)}) collective-permute-start(f32[4,8]{1,0:T(4,128)S(1)} %fusion.2), channel_id=1, source_target_pairs={{0,2},{1,3},{2,0},{3,1},{4,6},{5,7},{6,4},{7,5},{8,10},{9,11},{10,... | collective-permute-start | bytes 392 | tf_op jit(solution)/shard_map/ry/ppermute | solution.py:290
  128.6 1.2 collective-permute-start.21
  (10 other events, 68.9 us)
